TPU v7x, 32 devices: a whole 2x2x4 slice. The times are simulated.
32 devices in a mesh: occ: 4 (over z), vir: 8 (over y, x, core).
Axes of the slice: x: 2, y: 2, z: 4, core: 2. Of those that a mesh axis runs over, the one named last changes fastest.
Arguments:
- amplitudes: bfloat16 [40, 40, 400, 400], P('occ', None, 'vir'), may hold values from -6 to 6
- integrals: bfloat16 [400, 400, 3200], P('vir', 'occ'), may hold values from -0.109375 to 0.109375
- batch_index: int32 [1], replicated, may hold values from 0 to 49
- eps_occ: float32 [40], replicated, may hold values from -1 to -0.3
- eps_vir: float32 [400], replicated, may hold values from 0.2 to 1.5
Outputs:
- update: float32 [400, 400, 1600], P(None, 'vir', 'occ')
Inputs may be any that keep to these rules, and one draw needn't show every extreme that they name: Selects the virtual orbitals d from 8 * batch_index to 8 * batch_index + 7.
All inputs are finite; a program needn't handle non-finite values.
Results may differ from a plain program's by a relative error of at most 0.0029.
Values may be sent and summed in bfloat16 or wider, within the bound.
A program may use at most 384 MiB of HBM per device.

v0:
```python
import jax
import jax.numpy as jnp
from jax import lax
from jax.sharding import PartitionSpec as P

NB = 8


def shards(amplitudes, integrals, batch_index, eps_occ, eps_vir):
    occ_rows = amplitudes.shape[0]
    occ_all = amplitudes.shape[1]
    vir_local = amplitudes.shape[2]
    block_a = integrals.shape[0]
    block_b = integrals.shape[1]
    begin = batch_index[0] * NB
    sliced = lax.dynamic_slice_in_dim(amplitudes, begin, NB, 3)
    sliced = sliced.reshape(occ_rows, occ_all, vir_local * NB)
    weights_flat = integrals.reshape(block_a * block_b, integrals.shape[2])
    dims_last = (((1,), (1,)), ((), ()))
    columns = lax.all_gather(sliced, "vir", axis=2, tiled=True)
    columns = columns.reshape(occ_rows * occ_all, columns.shape[2])
    ladder = lax.dot_general(
        weights_flat,
        lax.all_gather(columns, "occ", axis=0, tiled=True),
        dims_last,
        preferred_element_type=jnp.float32,
    )
    ladder = 0.5 * ladder.reshape(block_a, block_b, occ_all, occ_all)
    mixed = (ladder - jnp.transpose(ladder, (0, 1, 3, 2))).astype(jnp.bfloat16)
    mixed = mixed.reshape(block_a, block_b, occ_all * occ_all)
    relaid = lax.all_to_all(
        lax.all_to_all(mixed, "occ", split_axis=2, concat_axis=1, tiled=True),
        "vir",
        split_axis=1,
        concat_axis=0,
        tiled=True,
    )
    returned = lax.all_to_all(relaid, "vir", split_axis=0, concat_axis=1, tiled=True)
    mirrored = jnp.swapaxes(returned, 0, 1)
    pair_count = relaid.shape[2]
    pair_rows = pair_count // occ_all
    width_b = relaid.shape[1]
    occ_index = lax.axis_index("occ")
    vir_index = lax.axis_index("vir")
    energy_rows = lax.dynamic_slice_in_dim(eps_occ, occ_index * pair_rows, pair_rows, 0)
    pair_energy = (energy_rows[:, None] + eps_occ[None, :]).reshape(pair_count)
    energy_cols = lax.dynamic_slice_in_dim(eps_vir, vir_index * width_b, width_b, 0)
    denominator = pair_energy[None, None, :] - eps_vir[:, None, None] - energy_cols[None, :, None]
    return (relaid.astype(jnp.float32) - mirrored.astype(jnp.float32)) / denominator


def solution(mesh):
    in_specs = (P("occ", None, "vir", None), P("vir", "occ", None), P(), P(), P())
    out_specs = P(None, "vir", "occ")
    return jax.shard_map(shards, mesh=mesh, in_specs=in_specs, out_specs=out_specs, check_vma=False)
```

profile of v0, /device:TPU:0, one launch (start us, length us, event | category | flops | bytes accessed | tf_op | source)
XLA Modules:
  0.0 1750.7 jit_solution(14106090877960667524)
XLA Ops:
  7.2 6.2 constant_dynamic-slice_fusion
  13.4 4.9 copy.30
  18.3 0.0 all-gather.3.cloned.1.call-update
  18.3 0.0 all-gather.5.cloned.1.call-start
  18.4 56.2 %all-gather.3.cloned.1.call-done = bf16[10,40,3200]{1,2,0:T(8,128)(2,1)} async-done(((bf16[10,40,400]{1,2,0:T(8,128)(2,1)}), bf16[10,40,3200]{1,2,0:T(8,128)(2,1)}) %all-gather.3.cloned.1.call-update) | async-done | bytes 2560016 | tf_op jit(solution)/shard_map/all_gather | solution.py:20
  74.6 8.3 copy.31
  82.9 0.0 all-gather.5.cloned.1.call-update
  82.9 33.5 %reshape.69 = bf16[5000,3200]{1,0:T(8,128)(2,1)} reshape(bf16[50,100,3200]{2,1,0:T(8,128)(2,1)} %param.6) | data formatting | bytes 64000000 | tf_op jit(solution)/shard_map/reshape | solution.py:18
  116.4 146.5 %all-gather.5.cloned.1.call-done = bf16[1600,3200]{1,0:T(8,128)(2,1)} async-done(((bf16[400,3200]{1,0:T(8,128)(2,1)}), bf16[1600,3200]{1,0:T(8,128)(2,1)}) %all-gather.5.cloned.1.call-update) | async-done | bytes 10240016 | tf_op jit(solution)/shard_map/all_gather | solution.py:24
  263.0 65.0 %multiply_bitcast_fusion = f32[5000,1600]{0,1:T(8,128)} fusion(bf16[1600,3200]{1,0:T(8,128)(2,1)} %all-gather.5.cloned.1.call-done, bf16[5000,3200]{1,0:T(8,128)(2,1)} %reshape.69), kind=kOutput, calls=%fused_computation.4 | convolution fusion | flops 51207999488 | bytes 74240000 | tf_op jit(solution)/shard_map/dot_general | solution.py:22
  327.9 43.7 %mul.29 = f32[50,100,40,40]{1,0,3,2:T(8,128)} reshape(f32[5000,1600]{0,1:T(8,128)} %multiply_bitcast_fusion) | data formatting | bytes 64000000 | tf_op jit(solution)/shard_map/mul | solution.py:28
  371.7 36.6 %fusion = bf16[50,100,40,40]{1,0,3,2:T(8,128)(2,1)} fusion(f32[50,100,40,40]{1,0,3,2:T(8,128)} %mul.29), kind=kLoop, calls=%fused_computation.1 | loop fusion | flops 16000000 | bytes 48000000 | tf_op jit(solution)/shard_map/convert_element_type | solution.py:29
  408.3 509.0 %all_to_all.45 = bf16[50,100,1600]{1,0,2:T(8,128)(2,1)} all-to-all(bf16[50,100,1600]{1,0,2:T(8,128)(2,1)} %bitcast.31), channel_id=1, replica_groups=mesh['occ'=4,'vir'=8] {'occ'}, dimensions={2} | all-to-all | bytes 32000000 | tf_op jit(solution)/shard_map/all_to_all | solution.py:32
  917.3 35.0 %copy.41 = bf16[50,100,4,400]{3,2,1,0:T(4,128)(2,1)} copy(bf16[50,100,4,400]{1,0,3,2:T(8,128)(2,1)} %bitcast.32) | data formatting | bytes 32000000 | tf_op jit(solution)/shard_map/all_to_all | solution.py:32
  952.3 15.0 copy.42
  967.3 253.9 %all_to_all.46 = bf16[50,400,400]{2,0,1:T(8,128)(2,1)} all-to-all(bf16[50,400,400]{2,0,1:T(8,128)(2,1)S(1)} %bitcast.33), channel_id=1, replica_groups=mesh['occ'=4,'vir'=8] {'vir'}, dimensions={1} | all-to-all | bytes 32000000 | tf_op jit(solution)/shard_map/all_to_all | solution.py:31
  1221.2 16.3 copy.37
  1237.5 29.7 %all_to_all.40 = bf16[400,50,400]{2,0,1:T(8,128)(2,1)} reshape(bf16[8,50,50,400]{3,1,0,2:T(8,128)(2,1)} %copy.37) | data formatting | bytes 32000000 | tf_op jit(solution)/shard_map/all_to_all | solution.py:31
  1267.2 30.0 %copy.38 = bf16[400,50,400]{2,1,0:T(8,128)(2,1)} copy(bf16[400,50,400]{2,0,1:T(8,128)(2,1)} %all_to_all.40) | data formatting | bytes 32000000 | tf_op jit(solution)/shard_map/all_to_all | solution.py:31
  1297.2 6.6 all-to-all-start.2
  1303.8 0.1 dynamic_slice.10
  1303.9 0.1 broadcast_add_fusion
  1304.0 0.1 add.34
  1304.1 0.0 copy-done
  1304.1 0.1 dynamic_slice.11
  1304.1 0.1 broadcast_subtract_fusion
  1304.3 249.2 %all-to-all-done.2 = bf16[400,50,400]{2,1,0:T(8,128)(2,1)} async-done(((bf16[400,50,400]{2,1,0:T(8,128)(2,1)}), bf16[400,50,400]{2,1,0:T(8,128)(2,1)}, u32[]{:S(2)}, u32[]{:S(2)}) %all-to-all-start.2) | async-done | bytes 16000032 | tf_op jit(solution)/shard_map/all_to_all | solution.py:38
  1553.5 24.7 %copy_convert_fusion = f32[400,50,400]{2,0,1:T(8,128)} fusion(bf16[400,50,400]{2,1,0:T(8,128)(2,1)} %all-to-all-done.2), kind=kLoop, calls=%fused_computation.5 | loop fusion | flops 8000000 | bytes 48000000 | tf_op jit(solution)/shard_map/convert_element_type | solution.py:49
  1578.2 41.8 %reshape.72 = f32[8,50,50,400]{3,1,0,2:T(8,128)} reshape(f32[400,50,400]{2,0,1:T(8,128)} %copy_convert_fusion) | data formatting | bytes 64000000 | tf_op jit(solution)/shard_map/convert_element_type | solution.py:49
  1620.0 48.8 %copy.40 = f32[50,8,50,400]{3,2,1,0:T(8,128)} copy(f32[50,8,50,400]{3,0,1,2:T(8,128)} %bitcast.30) | data formatting | bytes 64000000 | tf_op jit(solution)/shard_map/convert_element_type | solution.py:49
  1668.8 41.8 %reshape.71 = f32[50,400,400]{2,1,0:T(8,128)} reshape(f32[50,8,50,400]{3,2,1,0:T(8,128)} %copy.40) | data formatting | bytes 64000000 | tf_op jit(solution)/shard_map/convert_element_type | solution.py:49
  1710.6 33.2 %fusion.1 = f32[400,50,400]{2,0,1:T(8,128)} fusion(f32[50,400,400]{2,1,0:T(8,128)} %reshape.71, bf16[400,50,400]{2,0,1:T(8,128)(2,1)} %all_to_all.40, f32[50]{0:T(128)S(1)} %dynamic_slice.11, f32[400,400]{1,0:T(8,128)S(1)} %broadcast_subtract_fusion), kind=kLoop, calls=%fused_computation.3 | loop fusion | flops 32000000 | bytes 80640200 | tf_op jit(solution)/shard_map/div | solution.py:49
  (4 shorter events, 0.0 us)
Async XLA Ops:
  6.5 68.1 %all-gather.3.cloned.1.call-start = ((), (), s32[]{:S(2)}) async-start(), calls=%async_computation.3 | async-start | bytes 9216000 | tf_op jit(solution)/shard_map/all_gather | solution.py:20
  18.3 244.6 %all-gather.5.cloned.1.call-start = ((), (), s32[]{:S(2)}) async-start(), calls=%async_computation.4 | async-start | bytes 12800000 | tf_op jit(solution)/shard_map/all_gather | solution.py:24
  1297.2 6.6 copy-start.1
  1297.2 6.9 copy-start
  1297.2 256.3 %all-to-all-start.2 = ((bf16[400,50,400]{2,1,0:T(8,128)(2,1)}), bf16[400,50,400]{2,1,0:T(8,128)(2,1)}, u32[]{:S(2)}, u32[]{:S(2)}) async-start(bf16[400,50,400]{2,1,0:T(8,128)(2,1)} %copy.38), calls=%async_computation.2 | async-start | bytes 45875200 | tf_op jit(solution)/shard_map/all_to_all | solution.py:38
Sparse Core Ops, SparseCore 0:
  18.5 56.1 all-gather.2
  83.1 179.8 all-gather.4
where the time goes:
time: 1760 us; the launch traced here: 1750 us
  blocking collectives  763 us (43%)
  waiting for transfers between devices  452 us (26%)
  local copies, waits for them, and re-layouts  355 us (20%)
  other arithmetic  94.7 us (5%)
  matrix products  65 us (4%)
    all_to_all x1, blocking collectives, shards(): lax.all_to_all(mixed, 'occ', split_axis=2, concat_axis=1, tiled=True)  509 us
    all_to_all x1, blocking collectives, shards(): lax.all_to_all(lax.all_to_all(mixed, 'occ', split_axis=2, concat_axis=1,...  254 us
    all_to_all x1, waiting for transfers between devices, shards(): lax.all_to_all(relaid, 'vir', split_axis=0, concat_axis=1, tiled=True)  249 us
    all_gather x1, waiting for transfers between devices, shards(): lax.all_gather(columns, 'occ', axis=0, tiled=True)  147 us
    convert_element_type x3, local copies, waits for them, and re-layouts, shards(): mirrored.astype(jnp.float32)  132 us
    all_to_all x3, local copies, waits for them, and re-layouts, shards(): lax.all_to_all(lax.all_to_all(mixed, 'occ', split_axis=2, concat_axis=1,...  76 us
    dot_general x1, matrix products, shards(): lax.dot_general(weights_flat, lax.all_gather(columns, 'occ', axis=0, tile...  65 us
    all_gather x1, waiting for transfers between devices, shards(): columns = lax.all_gather(sliced, 'vir', axis=2, tiled=True)  56.2 us
  transfers between devices with their start and end apart: 3, of which 3 were waited for; matrix products, arithmetic and copies ran while one was open for 2% of the time, Pallas kernels for 0%

commit v1 on v0

--- a/solution.py
+++ b/solution.py
@@ -28,15 +28,9 @@
     ladder = 0.5 * ladder.reshape(block_a, block_b, occ_all, occ_all)
     mixed = (ladder - jnp.transpose(ladder, (0, 1, 3, 2))).astype(jnp.bfloat16)
     mixed = mixed.reshape(block_a, block_b, occ_all * occ_all)
-    relaid = lax.all_to_all(
-        lax.all_to_all(mixed, "occ", split_axis=2, concat_axis=1, tiled=True),
-        "vir",
-        split_axis=1,
-        concat_axis=0,
-        tiled=True,
-    )
-    returned = lax.all_to_all(relaid, "vir", split_axis=0, concat_axis=1, tiled=True)
-    mirrored = jnp.swapaxes(returned, 0, 1)
+    own_rows = lax.all_to_all(mixed, "occ", split_axis=2, concat_axis=1, tiled=True)
+    relaid = lax.all_to_all(own_rows, "vir", split_axis=1, concat_axis=0, tiled=True)
+    mirrored = jnp.swapaxes(own_rows, 0, 1)
     pair_count = relaid.shape[2]
     pair_rows = pair_count // occ_all
     width_b = relaid.shape[1]

time: 1760 us -> 1490 us (0.85)
  blocking collectives: 763 us -> 509 us
    all_to_all x1 -> x0, blocking collectives: 254 us -> none  [shards(): lax.all_to_all(lax.all_to_all(mixed, 'occ', split_axis=2, concat_axis=1,...]
    all_to_all x3 -> x0, local copies, waits for them, and re-layouts: 76 us -> none  [shards(): lax.all_to_all(lax.all_to_all(mixed, 'occ', split_axis=2, concat_axis=1,...]
    all_to_all x2 -> x4, local copies, waits for them, and re-layouts: 50 us -> 114 us  [shards(): lax.all_to_all(mixed, 'occ', split_axis=2, concat_axis=1, tiled=True)]
where the time goes in v1:
time: 1490 us; the launch traced here: 1480 us
  blocking collectives  509 us (34%)
  waiting for transfers between devices  452 us (30%)
  local copies, waits for them, and re-layouts  343 us (23%)
  other arithmetic  94.7 us (6%)
  matrix products  65 us (4%)
    all_to_all x1, blocking collectives, shards(): lax.all_to_all(mixed, 'occ', split_axis=2, concat_axis=1, tiled=True)  509 us
    all_to_all x1, waiting for transfers between devices, shards(): lax.all_to_all(own_rows, 'vir', split_axis=1, concat_axis=0, tiled=True)  249 us
    all_gather x1, waiting for transfers between devices, shards(): lax.all_gather(columns, 'occ', axis=0, tiled=True)  147 us
    convert_element_type x3, local copies, waits for them, and re-layouts, shards(): relaid.astype(jnp.float32) - mirrored.astype(jnp.float32)  132 us
    all_to_all x4, local copies, waits for them, and re-layouts, shards(): lax.all_to_all(mixed, 'occ', split_axis=2, concat_axis=1, tiled=True)  114 us
    dot_general x1, matrix products, shards(): lax.dot_general(weights_flat, lax.all_gather(columns, 'occ', axis=0, tile...  65 us
    all_gather x1, waiting for transfers between devices, shards(): columns = lax.all_gather(sliced, 'vir', axis=2, tiled=True)  56.2 us
    mul x1, local copies, waits for them, and re-layouts, shards(): ladder = 0.5 * ladder.reshape(block_a, block_b, occ_all, occ_all)  43.7 us
  transfers between devices with their start and end apart: 3, of which 3 were waited for; matrix products, arithmetic and copies ran while one was open for 2% of the time, Pallas kernels for 0%

profile of v1, /device:TPU:0, one launch (start us, length us, event | category | flops | bytes accessed | tf_op | source)
XLA Modules:
  0.0 1484.9 jit_solution(17963957135518208131)
XLA Ops:
  6.5 0.0 all-gather.3.cloned.1.call-start
  7.2 6.2 constant_dynamic-slice_fusion
  13.4 4.9 copy.27
  18.3 0.0 all-gather.3.cloned.1.call-update
  18.3 0.0 all-gather.5.cloned.1.call-start
  18.4 56.2 %all-gather.3.cloned.1.call-done = bf16[10,40,3200]{1,2,0:T(8,128)(2,1)} async-done(((bf16[10,40,400]{1,2,0:T(8,128)(2,1)}), bf16[10,40,3200]{1,2,0:T(8,128)(2,1)}) %all-gather.3.cloned.1.call-update) | async-done | bytes 2560016 | tf_op jit(solution)/shard_map/all_gather | solution.py:20
  74.6 8.3 copy.28
  82.9 0.0 all-gather.5.cloned.1.call-update
  82.9 33.5 %reshape.69 = bf16[5000,3200]{1,0:T(8,128)(2,1)} reshape(bf16[50,100,3200]{2,1,0:T(8,128)(2,1)} %param.6) | data formatting | bytes 64000000 | tf_op jit(solution)/shard_map/reshape | solution.py:18
  116.4 146.5 %all-gather.5.cloned.1.call-done = bf16[1600,3200]{1,0:T(8,128)(2,1)} async-done(((bf16[400,3200]{1,0:T(8,128)(2,1)}), bf16[1600,3200]{1,0:T(8,128)(2,1)}) %all-gather.5.cloned.1.call-update) | async-done | bytes 10240016 | tf_op jit(solution)/shard_map/all_gather | solution.py:24
  263.0 65.0 %multiply_bitcast_fusion = f32[5000,1600]{0,1:T(8,128)} fusion(bf16[1600,3200]{1,0:T(8,128)(2,1)} %all-gather.5.cloned.1.call-done, bf16[5000,3200]{1,0:T(8,128)(2,1)} %reshape.69), kind=kOutput, calls=%fused_computation.4 | convolution fusion | flops 51207999488 | bytes 74240000 | tf_op jit(solution)/shard_map/dot_general | solution.py:22
  327.9 43.7 %mul.29 = f32[50,100,40,40]{1,0,3,2:T(8,128)} reshape(f32[5000,1600]{0,1:T(8,128)} %multiply_bitcast_fusion) | data formatting | bytes 64000000 | tf_op jit(solution)/shard_map/mul | solution.py:28
  371.7 36.6 %fusion = bf16[50,100,40,40]{1,0,3,2:T(8,128)(2,1)} fusion(f32[50,100,40,40]{1,0,3,2:T(8,128)} %mul.29), kind=kLoop, calls=%fused_computation.1 | loop fusion | flops 16000000 | bytes 48000000 | tf_op jit(solution)/shard_map/convert_element_type | solution.py:29
  408.3 509.0 %all_to_all.27 = bf16[50,100,1600]{1,0,2:T(8,128)(2,1)} all-to-all(bf16[50,100,1600]{1,0,2:T(8,128)(2,1)} %bitcast.24), channel_id=1, replica_groups=mesh['occ'=4,'vir'=8] {'occ'}, dimensions={2} | all-to-all | bytes 32000000 | tf_op jit(solution)/shard_map/all_to_all | solution.py:31
  917.3 35.0 %copy.35 = bf16[50,100,4,400]{3,2,1,0:T(4,128)(2,1)} copy(bf16[50,100,4,400]{1,0,3,2:T(8,128)(2,1)} %bitcast.25) | data formatting | bytes 32000000 | tf_op jit(solution)/shard_map/all_to_all | solution.py:31
  952.3 20.3 %copy.31 = bf16[50,4,100,400]{3,2,1,0:T(8,128)(2,1)} copy(bf16[50,4,100,400]{3,1,2,0:T(4,128)(2,1)} %bitcast.26) | data formatting | bytes 32000000 | tf_op jit(solution)/shard_map/all_to_all | solution.py:31
  972.6 28.9 %all_to_all.23 = bf16[50,400,400]{2,1,0:T(8,128)(2,1)} reshape(bf16[50,4,100,400]{3,2,1,0:T(8,128)(2,1)} %copy.31) | data formatting | bytes 32000000 | tf_op jit(solution)/shard_map/all_to_all | solution.py:31
  1001.5 30.0 %copy.32 = bf16[50,400,400]{2,0,1:T(8,128)(2,1)} copy(bf16[50,400,400]{2,1,0:T(8,128)(2,1)} %all_to_all.23) | data formatting | bytes 32000000 | tf_op jit(solution)/shard_map/all_to_all | solution.py:31
  1031.4 6.4 all-to-all-start.1
  1037.8 0.0 copy-done.1
  1037.8 0.1 dynamic_slice.10
  1037.9 0.1 broadcast_add_fusion
  1038.0 0.1 add.34
  1038.1 0.0 copy-done
  1038.1 0.1 dynamic_slice.11
  1038.2 0.1 broadcast_subtract_fusion
  1038.3 249.5 %all-to-all-done.1 = bf16[50,400,400]{2,0,1:T(8,128)(2,1)} async-done(((bf16[50,400,400]{2,0,1:T(8,128)(2,1)}), bf16[50,400,400]{2,0,1:T(8,128)(2,1)}, u32[]{:S(2)}, u32[]{:S(2)}) %all-to-all-start.1) | async-done | bytes 16000032 | tf_op jit(solution)/shard_map/all_to_all | solution.py:32
  1287.8 24.7 %copy_convert_fusion = f32[50,400,400]{2,1,0:T(8,128)} fusion(bf16[50,400,400]{2,0,1:T(8,128)(2,1)} %all-to-all-done.1), kind=kLoop, calls=%fused_computation.5 | loop fusion | flops 8000000 | bytes 48000000 | tf_op jit(solution)/shard_map/convert_element_type | solution.py:43
  1312.4 41.8 %reshape.72 = f32[50,8,50,400]{3,2,1,0:T(8,128)} reshape(f32[50,400,400]{2,1,0:T(8,128)} %copy_convert_fusion) | data formatting | bytes 64000000 | tf_op jit(solution)/shard_map/convert_element_type | solution.py:43
  1354.2 48.8 %copy.34 = f32[8,50,50,400]{3,1,0,2:T(8,128)} copy(f32[8,50,50,400]{3,2,0,1:T(8,128)} %bitcast.23) | data formatting | bytes 64000000 | tf_op jit(solution)/shard_map/convert_element_type | solution.py:43
  1403.0 41.8 %reshape.71 = f32[400,50,400]{2,0,1:T(8,128)} reshape(f32[8,50,50,400]{3,1,0,2:T(8,128)} %copy.34) | data formatting | bytes 64000000 | tf_op jit(solution)/shard_map/convert_element_type | solution.py:43
  1444.8 33.2 %fusion.1 = f32[400,50,400]{2,0,1:T(8,128)} fusion(f32[400,50,400]{2,0,1:T(8,128)} %reshape.71, bf16[50,400,400]{2,1,0:T(8,128)(2,1)} %all_to_all.23, f32[50]{0:T(128)S(1)} %dynamic_slice.11, f32[400,400]{1,0:T(8,128)S(1)} %broadcast_subtract_fusion), kind=kLoop, calls=%fused_computation.3 | loop fusion | flops 32000000 | bytes 80640200 | tf_op jit(solution)/shard_map/div | solution.py:43
  (2 shorter events, 0.0 us)
Async XLA Ops:
  6.5 68.1 %all-gather.3.cloned.1.call-start = ((), (), s32[]{:S(2)}) async-start(), calls=%async_computation.2 | async-start | bytes 9216000 | tf_op jit(solution)/shard_map/all_gather | solution.py:20
  18.3 244.6 %all-gather.5.cloned.1.call-start = ((), (), s32[]{:S(2)}) async-start(), calls=%async_computation.3 | async-start | bytes 12800000 | tf_op jit(solution)/shard_map/all_gather | solution.py:24
  1031.4 6.4 copy-start.1
  1031.4 6.6 copy-start
  1031.4 256.3 %all-to-all-start.1 = ((bf16[50,400,400]{2,0,1:T(8,128)(2,1)}), bf16[50,400,400]{2,0,1:T(8,128)(2,1)}, u32[]{:S(2)}, u32[]{:S(2)}) async-start(bf16[50,400,400]{2,0,1:T(8,128)(2,1)} %copy.32), calls=%async_computation.1 | async-start | bytes 45875200 | tf_op jit(solution)/shard_map/all_to_all | solution.py:32
Sparse Core Ops, SparseCore 0:
  18.5 56.1 all-gather.2
  83.1 179.8 all-gather.4

commit v2 on v1

v2 whole, which is shorter than its diff:
```python
import functools

import jax
import jax.numpy as jnp
import numpy as np
from jax import lax
from jax.experimental import pallas as pl
from jax.experimental.pallas import tpu as pltpu
from jax.sharding import PartitionSpec as P

NB = 8
MESH = pl.DeviceIdType.MESH
VMEM_LIMIT = 60 * 1024 * 1024


def up(value, step):
    return -(-value // step) * step


def pair_tables(occ_all, occ_ranks):
    rows = occ_all // occ_ranks
    pairs = [(i, j) for i in range(occ_all) for j in range(i + 1, occ_all)]
    place = {pair: k for k, pair in enumerate(pairs)}
    count = up(len(pairs), 16)
    first = np.zeros((count,), np.int32)
    second = np.zeros((count,), np.int32)
    for k, (i, j) in enumerate(pairs):
        first[k], second[k] = i * occ_all + j, j * occ_all + i
    width = 0
    lists = []
    for owner in range(occ_ranks):
        mine = range(owner * rows, (owner + 1) * rows)
        lists.append([p for p in pairs if p[0] in mine or p[1] in mine])
        width = max(width, len(lists[-1]))
    width = up(width, 128)
    spread = np.zeros((count, occ_ranks * width), np.float32)
    expand = np.zeros((occ_ranks, width, up(rows * occ_all, 128)), np.float32)
    for owner, owned in enumerate(lists):
        low = owner * rows
        for k, (i, j) in enumerate(owned):
            spread[place[(i, j)], owner * width + k] = 1.0
            if low <= i < low + rows:
                expand[owner, k, (i - low) * occ_all + j] = 1.0
            if low <= j < low + rows:
                expand[owner, k, (j - low) * occ_all + i] = -1.0
    return first, second, spread, expand, count, width


def ladder_kernel(group, block_b, owners, width, w_ref, s_ref, t_ref, e_ref, out_ref):
    dims = (((1,), (1,)), ((), ()))
    weights = w_ref[...]
    left = lax.dot_general(weights, s_ref[...], dims, preferred_element_type=jnp.float32)
    right = lax.dot_general(weights, t_ref[...], dims, preferred_element_type=jnp.float32)
    mixed = (0.5 * left - 0.5 * right).astype(jnp.bfloat16)
    parts = jnp.dot(mixed, e_ref[...], preferred_element_type=jnp.float32)
    for owner in range(owners):
        for a in range(group):
            piece = parts[a * block_b : (a + 1) * block_b, owner * width : (owner + 1) * width]
            out_ref[owner, a, 0:block_b, :] = piece.astype(jnp.bfloat16)


def ladder_call(weights, first, second, spread, block_a, block_b, tall, owners, width):
    group = next(g for g in range(1, block_a + 1) if block_a % g == 0 and (g == block_a or g * block_b % 8 == 0))
    depth = weights.shape[1]
    count = first.shape[0]
    once = pl.Buffered(1)
    return pl.pallas_call(
        functools.partial(ladder_kernel, group, block_b, owners, width),
        grid=(block_a // group,),
        in_specs=[
            pl.BlockSpec((group * block_b, depth), lambda g: (g, 0)),
            pl.BlockSpec((count, depth), lambda g: (0, 0), pipeline_mode=once),
            pl.BlockSpec((count, depth), lambda g: (0, 0), pipeline_mode=once),
            pl.BlockSpec((count, owners * width), lambda g: (0, 0), pipeline_mode=once),
        ],
        out_specs=pl.BlockSpec((owners, group, tall, width), lambda g: (0, g, 0, 0)),
        out_shape=jax.ShapeDtypeStruct((owners, block_a, tall, width), jnp.bfloat16),
        compiler_params=pltpu.CompilerParams(vmem_limit_bytes=VMEM_LIMIT),
    )(weights, first, second, spread)


def exchange_kernel(occ_n, vir_n, pieces, step, starts, length, m_ref, r_ref, x_ref, hold, zs, zr, vs, vr, ls):
    occ = lax.axis_index("occ")
    vir = lax.axis_index("vir")
    ratio = vir_n // occ_n
    barrier = pltpu.get_barrier_semaphore()
    for k in range(1, occ_n):
        pl.semaphore_signal(barrier, inc=1, device_id={"occ": lax.rem(occ + k, occ_n)}, device_id_type=MESH)
    for k in range(1, vir_n):
        pl.semaphore_signal(barrier, inc=1, device_id={"vir": lax.rem(vir + k, vir_n)}, device_id_type=MESH)
    pl.semaphore_wait(barrier, occ_n - 1 + vir_n - 1)

    def z_copy(k, c):
        peer = lax.rem(occ + k, occ_n)
        rows = pl.ds(c * step, step)
        return pltpu.make_async_remote_copy(
            src_ref=m_ref.at[peer, rows],
            dst_ref=r_ref.at[occ, rows],
            send_sem=zs.at[k - 1, c],
            recv_sem=zr.at[k - 1, c],
            device_id={"occ": peer},
            device_id_type=MESH,
        )

    def forward(src_ref, quarter, k, c):
        rows = pl.ds(c * step, step)
        for h in range(ratio):
            target = quarter * ratio + h
            piece = src_ref.at[quarter, rows, pl.ds(starts[h], length)]

            @pl.when(target != vir)
            def _():
                pltpu.make_async_remote_copy(
                    src_ref=piece,
                    dst_ref=x_ref.at[vir, rows],
                    send_sem=vs.at[k, h, c],
                    recv_sem=vr.at[vir, c],
                    device_id={"vir": target},
                    device_id_type=MESH,
                ).start()

            @pl.when(target == vir)
            def _():
                into = pltpu.make_async_copy(piece, hold, ls.at[0])
                into.start()
                into.wait()
                out = pltpu.make_async_copy(hold, x_ref.at[vir, rows], ls.at[1])
                out.start()
                out.wait()

    for c in range(pieces):
        for k in range(1, occ_n):
            z_copy(k, c).start()
    for c in range(pieces):
        forward(m_ref, occ, 0, c)
        for k in range(1, occ_n):
            z_copy(k, c).wait_recv()
            forward(r_ref, lax.rem(occ + occ_n - k, occ_n), k, c)
    for c in range(pieces):
        rows = pl.ds(c * step, step)
        for k in range(1, occ_n):
            z_copy(k, c).wait_send()
        for k in range(occ_n):
            quarter = lax.rem(occ + occ_n - k, occ_n)
            for h in range(ratio):
                target = quarter * ratio + h

                @pl.when(target != vir)
                def _():
                    pltpu.make_async_remote_copy(
                        src_ref=x_ref.at[vir, rows],
                        dst_ref=x_ref.at[vir, rows],
                        send_sem=vs.at[k, h, c],
                        recv_sem=vr.at[vir, c],
                        device_id={"vir": target},
                        device_id_type=MESH,
                    ).wait_send()

        for k in range(1, vir_n):
            source = lax.rem(vir + k, vir_n)
            pltpu.make_async_remote_copy(
                src_ref=x_ref.at[source, rows],
                dst_ref=x_ref.at[source, rows],
                send_sem=vs.at[0, 0, c],
                recv_sem=vr.at[source, c],
                device_id={"vir": source},
                device_id_type=MESH,
            ).wait_recv()


def exchange_call(terms, vir_n, starts, length):
    occ_n, block_a, tall, width = terms.shape
    pieces = 5
    step = block_a // pieces
    ratio = vir_n // occ_n
    anywhere = pl.BlockSpec(memory_space=pl.ANY)
    return pl.pallas_call(
        functools.partial(exchange_kernel, occ_n, vir_n, pieces, step, starts, length),
        in_specs=[anywhere],
        out_specs=[anywhere, anywhere],
        out_shape=[
            jax.ShapeDtypeStruct(terms.shape, terms.dtype),
            jax.ShapeDtypeStruct((vir_n, block_a, length, width), terms.dtype),
        ],
        scratch_shapes=[
            pltpu.VMEM((step, length, width), terms.dtype),
            pltpu.SemaphoreType.DMA((occ_n - 1, pieces)),
            pltpu.SemaphoreType.DMA((occ_n - 1, pieces)),
            pltpu.SemaphoreType.DMA((occ_n, ratio, pieces)),
            pltpu.SemaphoreType.DMA((vir_n, pieces)),
            pltpu.SemaphoreType.DMA((2,)),
        ],
        compiler_params=pltpu.CompilerParams(collective_id=0, has_side_effects=True, vmem_limit_bytes=16 * 1024 * 1024),
    )(terms)


def combine_kernel(sub, shifts, quarter_rows, where, ev_ref, m_ref, r_ref, x_ref, e_ref, pair_ref, eb_ref, out_ref, *mirror):
    k, s = pl.program_id(0), pl.program_id(1)
    count_b, tall, width = m_ref.shape[1:]
    out_b, pair_count = out_ref.shape[1:]
    expand = e_ref[...]

    def fill(ref):
        def body(b, _):
            whole = jnp.dot(ref[0, b], expand, preferred_element_type=jnp.float32)
            for n, lanes in enumerate(mirror):
                lanes[pl.ds(pl.multiple_of(b * tall, 8), tall), :] = whole[:, n * 128 : (n + 1) * 128]
            return 0

        lax.fori_loop(0, count_b, body, 0)

    @pl.when(jnp.logical_and(s == 0, k == 0))
    def _():
        fill(m_ref)

    @pl.when(jnp.logical_and(s == 0, k > 0))
    def _():
        fill(r_ref)

    base = s * sub
    half = where[1]
    first_a = (where[0] + k) % pl.num_programs(0) * quarter_rows + base

    def row(i, _):
        whole = jnp.dot(x_ref[0, i], expand, preferred_element_type=jnp.float32)
        direct = whole[shifts[0] : shifts[0] + out_b]
        for h in range(1, len(shifts)):
            direct = jnp.where(half == h, whole[shifts[h] : shifts[h] + out_b], direct)
        back = jnp.concatenate([lanes[pl.ds(base + i, out_b, stride=tall), :] for lanes in mirror], axis=1)
        denominator = pair_ref[...] - ev_ref[first_a + i] - eb_ref[...]
        out_ref[i] = (direct - back)[:, :pair_count] / denominator
        return 0

    lax.fori_loop(0, sub, row, 0)


def combine_call(where, eps_vir, terms, own, relaid, expand, pair_energy, energy_b, block_a, ratio, starts):
    occ_n, _, tall, width = terms.shape
    vir_n, _, length, _ = relaid.shape
    sub = block_a // 5
    steps = ratio * 5
    out_b = block_a
    pair_count = pair_energy.shape[1]
    lanes = expand.shape[1]
    shifts = tuple(h * out_b - starts[h] for h in range(ratio))

    def peer(k, w):
        return (w[0] + k) % occ_n

    spec = pltpu.PrefetchScalarGridSpec(
        num_scalar_prefetch=2,
        grid=(occ_n, steps),
        in_specs=[
            pl.BlockSpec((1, block_a, tall, width), lambda k, s, w, ev: (w[0], 0, 0, 0), pipeline_mode=pl.Buffered(1)),
            pl.BlockSpec((1, block_a, tall, width), lambda k, s, w, ev: (peer(jnp.maximum(k, 1), w), 0, 0, 0)),
            pl.BlockSpec((1, sub, length, width), lambda k, s, w, ev: (peer(k, w) * ratio + s // 5, s % 5, 0, 0)),
            pl.BlockSpec((width, lanes), lambda k, s, w, ev: (0, 0)),
            pl.BlockSpec((1, pair_count), lambda k, s, w, ev: (0, 0)),
            pl.BlockSpec((out_b, 1), lambda k, s, w, ev: (0, 0)),
        ],
        out_specs=pl.BlockSpec((sub, out_b, pair_count), lambda k, s, w, ev: (peer(k, w) * steps + s, 0, 0)),
        scratch_shapes=[pltpu.VMEM((block_a * tall, 128), jnp.float32)] * (lanes // 128),
    )
    return pl.pallas_call(
        functools.partial(combine_kernel, sub, shifts, ratio * block_a),
        grid_spec=spec,
        out_shape=jax.ShapeDtypeStruct((vir_n * block_a, out_b, pair_count), jnp.float32),
        compiler_params=pltpu.CompilerParams(vmem_limit_bytes=VMEM_LIMIT),
    )(where, eps_vir, terms, own, relaid, expand, pair_energy, energy_b)


def shards(occ_n, vir_n, amplitudes, integrals, batch_index, eps_occ, eps_vir):
    occ_rows, occ_all, vir_local = amplitudes.shape[:3]
    block_a, block_b, depth = integrals.shape
    ratio = block_b // block_a
    pair_count = occ_rows * occ_all
    starts = tuple(h * block_a // 8 * 8 for h in range(ratio))
    length = max(up((h + 1) * block_a, 8) - starts[h] for h in range(ratio))
    tall = max(up(block_b, 8), max(s + length for s in starts))
    first, second, spread, expand, count, width = pair_tables(occ_all, occ_n)
    occ_index = lax.axis_index("occ")
    vir_index = lax.axis_index("vir")

    sliced = lax.dynamic_slice_in_dim(amplitudes, batch_index[0] * NB, NB, 3)
    sliced = sliced.reshape(pair_count, vir_local * NB)
    columns = lax.all_gather(sliced, "occ", axis=0, tiled=True)
    selected = lax.all_gather(columns, "vir", axis=1, tiled=True)
    weights = integrals.reshape(block_a * block_b, depth)
    terms = ladder_call(
        weights,
        jnp.take(selected, first, axis=0),
        jnp.take(selected, second, axis=0),
        jnp.asarray(spread, jnp.bfloat16),
        block_a,
        block_b,
        tall,
        occ_n,
        width,
    )
    own, relaid = exchange_call(terms, vir_n, starts, length)
    energy_rows = lax.dynamic_slice_in_dim(eps_occ, occ_index * occ_rows, occ_rows, 0)
    pair_energy = (energy_rows[:, None] + eps_occ[None, :]).reshape(1, pair_count)
    energy_b = lax.dynamic_slice_in_dim(eps_vir, vir_index * block_a, block_a, 0).reshape(block_a, 1)
    mine = lax.dynamic_index_in_dim(jnp.asarray(expand, jnp.bfloat16), occ_index, 0, keepdims=False)
    where = jnp.stack([occ_index, vir_index % ratio]).astype(jnp.int32)
    return combine_call(where, eps_vir, terms, own, relaid, mine, pair_energy, energy_b, block_a, ratio, starts)


def solution(mesh):
    in_specs = (P("occ", None, "vir", None), P("vir", "occ", None), P(), P(), P())
    out_specs = P(None, "vir", "occ")
    body = functools.partial(shards, mesh.shape["occ"], mesh.shape["vir"])
    return jax.shard_map(body, mesh=mesh, in_specs=in_specs, out_specs=out_specs, check_vma=False)
```

time: 1490 us -> 881 us (0.59)
  Pallas kernels: 0 us -> 627 us
  blocking collectives: 509 us -> 0 us
  waiting for transfers between devices: 452 us -> 65.6 us
  local copies, waits for them, and re-layouts: 343 us -> 156 us
  other arithmetic: 94.7 us -> 0.67 us
  matrix products: 65 us -> 0 us
    pallas_call x0 -> x3, Pallas kernels: none -> 627 us  [the longest x1 373 us: exchange_call(): pl.pallas_call(functools.partial(exchange_kernel, occ_n, vir_n, pieces, s...]
    all_to_all x1 -> x0, blocking collectives: 509 us -> none  [shards(): lax.all_to_all(mixed, 'occ', split_axis=2, concat_axis=1, tiled=True)]
    all_to_all x1 -> x0, waiting for transfers between devices: 249 us -> none  [shards(): lax.all_to_all(own_rows, 'vir', split_axis=1, concat_axis=0, tiled=True)]
    all_gather x2, waiting for transfers between devices: 203 us -> 65.6 us  [the longest x1 40.8 us: shards(): columns = lax.all_gather(sliced, 'occ', axis=0, tiled=True)]
    convert_element_type x3 -> x0, local copies, waits for them, and re-layouts: 132 us -> none  [shards(): relaid.astype(jnp.float32) - mirrored.astype(jnp.float32)]
    all_to_all x4 -> x0, local copies, waits for them, and re-layouts: 114 us -> none  [shards(): lax.all_to_all(mixed, 'occ', split_axis=2, concat_axis=1, tiled=True)]
    dot_general x1 -> x0, matrix products: 65 us -> none  [shards(): lax.dot_general(weights_flat, lax.all_gather(columns, 'occ', axis=0, tile...]
    convert_element_type x2 -> x0, other arithmetic: 61.3 us -> none  [the longest x1 36.6 us: shards(): mixed = (ladder - jnp.transpose(ladder, (0, 1, 3, 2))).astype(jnp.bfloat16)]
  transfers between devices with their start and end apart: 3 -> 2, of which waited for: 3 -> 2; matrix products, arithmetic and copies ran while one was open for 2% -> 4% of each run, Pallas kernels for 0% -> 0%
where the time goes in v2:
time: 881 us; the launch traced here: 864 us
  Pallas kernels  627 us (71%)
  local copies, waits for them, and re-layouts  156 us (18%)
  waiting for transfers between devices  65.6 us (7%)
  between operations  14.1 us (2%)
    pallas_call x1, Pallas kernels, exchange_call(): pl.pallas_call(functools.partial(exchange_kernel, occ_n, vir_n, pieces, s...  373 us
    pallas_call x1, Pallas kernels, combine_call(): pl.pallas_call(functools.partial(combine_kernel, sub, shifts, ratio * blo...  141 us
    pallas_call x1, Pallas kernels, ladder_call(): pl.pallas_call(functools.partial(ladder_kernel, group, block_b, owners, w...  113 us
    all_gather x1, waiting for transfers between devices, shards(): columns = lax.all_gather(sliced, 'occ', axis=0, tiled=True)  40.8 us
    pallas_call x1, local copies, waits for them, and re-layouts, combine_call(): pl.pallas_call(functools.partial(combine_kernel, sub, shifts, ratio * blo...  38.9 us
    reshape x1, local copies, waits for them, and re-layouts, shards(): weights = integrals.reshape(block_a * block_b, depth)  33.3 us
    all_gather x1, waiting for transfers between devices, shards(): selected = lax.all_gather(columns, 'vir', axis=1, tiled=True)  24.8 us
  transfers between devices with their start and end apart: 2, of which 2 were waited for; matrix products, arithmetic and copies ran while one was open for 4% of the time, Pallas kernels for 0%

profile of v2, /device:TPU:0, one launch (start us, length us, event | category | flops | bytes accessed | tf_op | source)
XLA Modules:
  0.0 863.5 jit_solution(6840729019865411760)
XLA Ops:
  6.5 0.0 all-gather.3.cloned.1.call-start
  7.2 6.2 constant_dynamic-slice_fusion
  13.4 5.5 copy.22
  18.8 0.0 copy-start.4
  18.8 1.2 reshape.42
  20.1 0.9 copy.23
  21.0 0.0 all-gather.3.cloned.1.call-update
  21.0 0.2 all-gather.5.cloned.1.call-start
  21.3 40.8 %all-gather.3.cloned.1.call-done = bf16[1600,400]{1,0:T(8,128)(2,1)} async-done(((bf16[400,400]{1,0:T(8,128)(2,1)}), bf16[1600,400]{1,0:T(8,128)(2,1)}) %all-gather.3.cloned.1.call-update) | async-done | bytes 1280016 | tf_op jit(solution)/shard_map/all_gather | solution.py:286
  62.0 3.5 copy.24
  65.5 0.0 all-gather.5.cloned.1.call-update
  65.5 0.0 copy-done.4
  65.6 0.1 dynamic_slice.15
  65.6 0.1 broadcast_add_fusion
  65.7 0.7 add.53.pair_ref
  66.4 0.8 dynamic-slice_bitcast_fusion.1
  67.1 0.7 copy.27.eb_ref
  67.9 33.3 %reshape.41.w_ref = bf16[5000,3200]{1,0:T(8,128)(2,1)} reshape(bf16[50,100,3200]{2,1,0:T(8,128)(2,1)} %param.12) | data formatting | bytes 64000000 | tf_op jit(solution)/shard_map/reshape | solution.py:288
  101.1 0.6 pad_add_fusion.where
  101.7 0.0 copy-done.3
  101.8 1.8 dynamic-slice_bitcast_fusion.e_ref
  103.6 24.8 %all-gather.5.cloned.1.call-done = bf16[1600,3200]{0,1:T(8,128)(2,1)} async-done(((bf16[1600,400]{0,1:T(8,128)(2,1)}), bf16[1600,3200]{0,1:T(8,128)(2,1)}) %all-gather.5.cloned.1.call-update) | async-done | bytes 10240016 | tf_op jit(solution)/shard_map/all_gather | solution.py:287
  128.4 15.8 %copy.25 = bf16[1600,3200]{1,0:T(8,128)(2,1)} copy(bf16[1600,3200]{0,1:T(8,128)(2,1)} %all-gather.5.cloned.1.call-done) | data formatting | bytes 20480000 | tf_op jit(solution)/shard_map/all_gather | solution.py:287
  144.1 17.5 %gather_fusion.1 = bf16[784,3200]{1,0:T(8,128)(2,1)} fusion(bf16[1600,3200]{1,0:T(8,128)(2,1)} %copy.25, s32[1024]{0:T(1024)S(1)} %pad_clamp_fusion), kind=kCustom, calls=%fused_computation.1.clone | custom fusion | bytes 10038336 | tf_op jit(solution)/shard_map/jit(_take)/gather | solution.py:292
  161.6 17.5 %gather_fusion = bf16[784,3200]{1,0:T(8,128)(2,1)} fusion(bf16[1600,3200]{1,0:T(8,128)(2,1)} %copy.25, s32[1024]{0:T(1024)S(1)} %pad_clamp_fusion.1), kind=kCustom, calls=%fused_computation.clone | custom fusion | bytes 10038336 | tf_op jit(solution)/shard_map/jit(_take)/gather | solution.py:291
  179.2 113.1 %shard_map.91.m_ref = bf16[4,50,104,384]{3,2,1,0:T(8,128)(2,1)} custom-call(bf16[5000,3200]{1,0:T(8,128)(2,1)} %reshape.41.w_ref, bf16[784,3200]{1,0:T(8,128)(2,1)} %gather_fusion, bf16[784,3200]{1,0:T(8,128)(2,1)} %gather_fusion.1, bf16[784,1536]{1,0:T(8,128)(2,1)} %constant.58.clone.e_ref), custom_call_target="tpu_custom_call" | custom-call | tf_op jit(solution)/shard_map/pallas_call | solution.py:67
  292.3 5.5 copy-done
  297.8 373.2 %shard_map.92 = (bf16[4,50,104,384]{3,2,1,0:T(8,128)(2,1)S(1)}, bf16[8,50,56,384]{3,2,1,0:T(8,128)(2,1)}) custom-call(bf16[4,50,104,384]{3,2,1,0:T(8,128)(2,1)S(1)} %copy-done), custom_call_target="tpu_custom_call" | custom-call | tf_op jit(solution)/shard_map/pallas_call | solution.py:177
  671.1 0.0 copy-start.1
  671.1 5.9 copy-done.1
  677.0 140.8 %shard_map.93 = f32[400,50,400]{2,1,0:T(8,128)} custom-call(s32[2]{0:T(128)} %pad_add_fusion.where, f32[400]{0:T(512)} %ev_ref.1, bf16[4,50,104,384]{3,2,1,0:T(8,128)(2,1)} %shard_map.91.m_ref, bf16[4,50,104,384]{3,2,1,0:T(8,128)(2,1)} %copy-done.1, bf16[8,50,56,384]{3,2,1,0:T(8,128)(2,1)} %get-tuple-element.9.x_ref, ...), custom_call_target="tpu_custom_call" | custom-call | tf_op jit(solution)/shard_map/pallas_call | solution.py:264
  817.8 38.9 %copy.28 = f32[400,50,400]{2,0,1:T(8,128)} copy(f32[400,50,400]{2,1,0:T(8,128)} %shard_map.93) | data formatting | bytes 64000000 | tf_op jit(solution)/shard_map/pallas_call | solution.py:264
  (6 shorter events, 0.0 us)
Async XLA Ops:
  6.5 55.5 %all-gather.3.cloned.1.call-start = ((), (), s32[]{:S(2)}) async-start(), calls=%async_computation | async-start | bytes 2048000 | tf_op jit(solution)/shard_map/all_gather | solution.py:286
  18.8 46.7 %copy-start.4 = (f32[40]{0:T(128)S(1)}, f32[40]{0:T(128)}, u32[]{:S(2)}) copy-start(f32[40]{0:T(128)} %param.14) | copy-start | bytes 484
  21.0 107.3 %all-gather.5.cloned.1.call-start = ((), (), s32[]{:S(2)}) async-start(), calls=%async_computation.1 | async-start | bytes 11980800 | tf_op jit(solution)/shard_map/all_gather | solution.py:287
  67.9 33.9 %copy-start.3 = (s32[784]{0:T(1024)S(1)}, s32[784]{0:T(1024)}, u32[]{:S(2)}) copy-start(s32[784]{0:T(1024)} %constant.80) | copy-start | bytes 9412
  67.9 33.9 %copy-start.2 = (s32[784]{0:T(1024)S(1)}, s32[784]{0:T(1024)}, u32[]{:S(2)}) copy-start(s32[784]{0:T(1024)} %constant.81) | copy-start | bytes 9412
  292.3 5.5 copy-start
  671.1 5.9 copy-start.1
Sparse Core Ops, SparseCore 0:
  21.2 40.8 all-gather.2
  65.7 62.6 all-gather.4
